TPU v7x, 32 devices: a whole 2x2x4 slice. The times are simulated.
32 devices in a mesh: prow: 4 (over z), pcol: 8 (over y, x, core).
Axes of the slice: x: 2, y: 2, z: 4, core: 2. Of those that a mesh axis runs over, the one named last changes fastest.
Arguments:
- anc_inverse: float32 [2048, 2048], P('pcol', 'prow')
- pattern_one: int32 [8, 4], replicated, may hold values from 0 to 7, as said below
- parents: int32 [8], replicated, may hold values from 0 to 7, as said below
- low_one: float32 [8, 1024, 256], P('pcol', 'prow'), may hold values from -2 to 2
- pivot_one: float32 [8, 256, 256], P('pcol'), may hold values from -4 to 4
- low_two: float32 [8, 1024, 256], P('pcol', 'prow'), may hold values from -2 to 2
- second_scaled_factor: float32 [8, 256, 256], P('pcol'), may hold values from -2 to 2
- second_pivot_inverse: float32 [8, 256, 256], P('pcol'), may hold values from -4 to 4
Outputs:
- column_one: float32 [8, 2048, 256], P('prow', 'pcol')
- diag_one: float32 [8, 256, 256], P('pcol')
- column_two: float32 [8, 2048, 256], P('prow', 'pcol')
- second_parent_inverse: float32 [8, 256, 256], P('pcol')
- second_diagonal_inverse: float32 [8, 256, 256], P('pcol')
Inputs may be any that keep to these rules, and one draw needn't show every extreme that they name: `pattern_one`: entry r of each row names an ancestor of process row r: it lies in r * 2 to r * 2 + 1; for each r, every ancestor of that range is entry r of exactly 4 rows. `parents`: every first-level supernode is the parent of exactly one second-level supernode.
All inputs are finite; a program needn't handle non-finite values.
Results may differ from a plain program's by a relative error of at most 0.000073.
Values sent between devices are 32-bit elements; how exact they have to be, the bound alone decides.
A program may use at most 128 MiB of HBM per device.

v0:
```python
import jax
import jax.numpy as jnp
from jax import lax
from jax.sharding import PartitionSpec as P


def batched(left, right):
    return jnp.einsum("kab,kbd->kad", left, right, precision=lax.Precision.HIGHEST)


def batched_left_t(left, right):
    return jnp.einsum("kba,kbd->kad", left, right, precision=lax.Precision.HIGHEST)


def pick_rows(hit_mask, count):
    total = hit_mask.shape[0]
    keys = jnp.where(hit_mask, 0, total).astype(jnp.int32) + jnp.arange(total, dtype=jnp.int32)
    chosen_rows = jnp.argsort(keys)[:count]
    valid = jnp.take(hit_mask, chosen_rows, axis=0).astype(jnp.float32)[:, None, None]
    return (chosen_rows, valid)


def body(
    anc_inverse,
    pattern_one,
    parents,
    low_one,
    pivot_one,
    low_two,
    second_scaled_factor,
    second_pivot_inverse,
):
    my_row = lax.axis_index("prow")
    my_col = lax.axis_index("pcol")
    row_count = lax.axis_size("prow")
    col_count = lax.axis_size("pcol")
    per_row_anc = col_count // row_count
    supernode_block_width = pivot_one.shape[1]
    per_col_one = pivot_one.shape[0]
    per_col_two = second_scaled_factor.shape[0]
    owned = anc_inverse.shape[1] // supernode_block_width
    zblocks = anc_inverse.reshape(supernode_block_width, owned, supernode_block_width).transpose(
        1, 0, 2
    )
    lowall = lax.all_gather(low_one, "pcol", axis=0, tiled=True)
    total_one = lowall.shape[0]
    owned_slot_list = lax.dynamic_index_in_dim(pattern_one, my_row, 1, keepdims=False)
    chosen = jnp.take(zblocks, owned_slot_list - my_row * owned, axis=0)
    first_terms = batched(chosen, lowall)
    lowsec, topall = (
        lax.all_gather(low_two, "pcol", axis=0, tiled=True),
        lax.all_gather(second_scaled_factor, "pcol", axis=0, tiled=True),
    )
    total_two = lowsec.shape[0]
    pattern_two = jnp.take(pattern_one, parents, axis=0)
    my_slots_two = lax.dynamic_index_in_dim(pattern_two, my_row, 1, keepdims=False)
    chosen_two = jnp.take(zblocks, my_slots_two - my_row * owned, axis=0)
    first_full = -lax.psum(first_terms, "prow")
    share = total_two // row_count
    start = my_row * share
    parents_share = lax.dynamic_slice_in_dim(parents, start, share, 0)
    tops_share = lax.dynamic_slice_in_dim(topall, start, share, 0)
    carried = batched(jnp.take(first_full, parents_share, axis=0), tops_share)
    base_terms = batched(chosen_two, lowsec)
    updated = lax.dynamic_slice_in_dim(base_terms, start, share, 0) + carried
    second_terms = lax.dynamic_update_slice_in_dim(base_terms, updated, start, 0)
    second_full = -lax.psum(second_terms, "prow")
    rows_one, valid_one = pick_rows(owned_slot_list == my_col, total_one // per_row_anc)
    pivot_small = valid_one * batched_left_t(
        jnp.take(lowall, rows_one, axis=0), jnp.take(first_full, rows_one, axis=0)
    )
    pivot_terms = jnp.zeros_like(first_full).at[rows_one].add(pivot_small)
    pivot_part = lax.psum_scatter(pivot_terms, "pcol", scatter_dimension=0, tiled=True)
    pivot_sum = lax.psum(pivot_part, "prow")
    diag_one = pivot_one - pivot_sum
    count_one = first_full.shape[0] // row_count
    column_one = lax.dynamic_slice_in_dim(first_full, my_row * count_one, count_one, 0)
    second_level_count = second_full.shape[0] // row_count
    column_two = lax.dynamic_slice_in_dim(
        second_full, my_row * second_level_count, second_level_count, 0
    )
    rows_two, valid_two = pick_rows(my_slots_two == my_col, total_two // per_row_anc)
    lows_picked = jnp.take(lowsec, rows_two, axis=0)
    parent_picked = jnp.take(first_full, jnp.take(parents, rows_two, axis=0), axis=0)
    cross_small = valid_two * batched_left_t(parent_picked, lows_picked)
    diag_small = valid_two * batched_left_t(lows_picked, jnp.take(second_full, rows_two, axis=0))
    local_parent = parents - my_col * per_col_one
    own_parent = (local_parent >= 0) & (local_parent < per_col_one)
    rows_own, valid_own = pick_rows(own_parent, per_col_two)
    valid_own = valid_own * (my_row == 0).astype(jnp.float32)
    local_picked = jnp.clip(jnp.take(local_parent, rows_own, axis=0), 0, per_col_one - 1)
    picked = jnp.take(diag_one, local_picked, axis=0)
    own_small = valid_own * batched(picked, jnp.take(topall, rows_own, axis=0))
    cross_terms = (
        jnp.zeros_like(second_full).at[rows_two].add(cross_small).at[rows_own].add(own_small)
    )
    diag_terms = jnp.zeros_like(second_full).at[rows_two].add(diag_small)
    part_cross, part_diag = (
        lax.psum_scatter(cross_terms, "pcol", scatter_dimension=0, tiled=True),
        lax.psum_scatter(diag_terms, "pcol", scatter_dimension=0, tiled=True),
    )
    sum_cross, sum_diag = lax.psum((part_cross, part_diag), "prow")
    second_parent_inverse = -sum_cross
    second_diagonal_inverse = (
        second_pivot_inverse
        - batched_left_t(second_scaled_factor, second_parent_inverse)
        - sum_diag
    )
    return (column_one, diag_one, column_two, second_parent_inverse, second_diagonal_inverse)


def solution(mesh):
    placed = (
        P("pcol", "prow"),
        P(),
        P(),
        P("pcol", "prow", None),
        P("pcol", None, None),
        P("pcol", "prow", None),
        P("pcol", None, None),
        P("pcol", None, None),
    )
    return jax.shard_map(
        body,
        mesh=mesh,
        in_specs=placed,
        out_specs=(
            P("prow", "pcol", None),
            P("pcol", None, None),
            P("prow", "pcol", None),
            P("pcol", None, None),
            P("pcol", None, None),
        ),
        check_vma=False,
    )
```

profile of v0, /device:TPU:0, one launch (start us, length us, event | category | flops | bytes accessed | tf_op | source)
XLA Modules:
  0.0 471.5 jit_solution(3958737760766188225)
XLA Ops:
  10.5 30.0 %all-gather.4.cloned.1.call-done = f32[8,256,256]{2,1,0:T(8,128)} async-done(((f32[1,256,256]{2,1,0:T(8,128)}), f32[8,256,256]{2,1,0:T(8,128)}) %all-gather.4.cloned.1.call-update) | async-done | bytes 2097168 | tf_op jit(solution)/shard_map/all_gather | solution.py:45
  40.4 5.1 %fusion.2 = f32[8,256,256]{2,1,0:T(8,128)} fusion(f32[8,256,256]{2,1,0:T(8,128)} %all-gather.4.cloned.1.call-done, f32[8,256,256]{2,1,0:T(8,128)S(1)} %gather_fusion.3, pred[8]{0:T(512)(128)(4,1)S(1)} %compare_and_fusion.4), kind=kOutput, calls=%fused_computation.17 | convolution fusion | flops 1611137024 | bytes 6291464 | tf_op jit(solution)/shard_map/kab,kbd->kad/dot_general | solution.py:8
  48.7 1.7 gather_fusion.5
  50.4 81.4 %all-reduce.6.cloned.1.call-done = f32[8,256,256]{2,1,0:T(8,128)} async-done(((f32[8,256,256]{2,1,0:T(8,128)}), f32[8,256,256]{2,1,0:T(8,128)}) %all-reduce.6.cloned.1.call-update) | async-done | bytes 2097168 | tf_op jit(solution)/shard_map/psum | solution.py:58
  131.8 1.8 neg.9
  133.6 1.7 gather_fusion.6
  135.3 4.5 convolution_multiply_fusion.2
  140.0 2.3 scatter_fusion
  142.3 1.3 copy-done.3
  144.8 2.0 gather_fusion.7
  146.9 13.7 %all-gather.6.cloned.1.call-done = f32[8,256,256]{2,1,0:T(8,128)} async-done(((f32[1,256,256]{2,1,0:T(8,128)}), f32[8,256,256]{2,1,0:T(8,128)}) %all-gather.6.cloned.1.call-update) | async-done | bytes 2097168 | tf_op jit(solution)/shard_map/all_gather | solution.py:51
  160.6 5.8 %fusion = f32[8,256,256]{2,1,0:T(8,128)} fusion(f32[8,256,256]{2,1,0:T(8,128)} %all-gather.6.cloned.1.call-done, f32[8,256,256]{2,1,0:T(8,128)} %gather_fusion.7, pred[8]{0:T(512)(128)(4,1)S(1)} %compare_and_fusion.2), kind=kOutput, calls=%fused_computation.15 | convolution fusion | flops 1611137024 | bytes 6291464 | tf_op jit(solution)/shard_map/kab,kbd->kad/dot_general | solution.py:8
  166.9 23.2 %all-gather.8.cloned.1.call-done = f32[8,256,256]{2,1,0:T(8,128)} async-done(((f32[1,256,256]{2,1,0:T(8,128)}), f32[8,256,256]{2,1,0:T(8,128)}) %all-gather.8.cloned.1.call-update) | async-done | bytes 2097168 | tf_op jit(solution)/shard_map/all_gather | solution.py:52
  190.1 2.7 fusion.4
  192.9 41.5 %reduce-scatter.4.cloned.1.call-done = f32[1,256,256]{2,1,0:T(8,128)} async-done(((f32[8,256,256]{2,1,0:T(8,128)}), f32[1,256,256]{2,1,0:T(8,128)}) %reduce-scatter.4.cloned.1.call-update) | async-done | bytes 262160 | tf_op jit(solution)/shard_map/reduce_scatter | solution.py:73
  241.2 2.6 gather_fusion.10
  243.8 1.6 gather_fusion.9
  245.3 4.2 convolution_multiply_fusion.1
  249.8 2.3 scatter_fusion.1
  252.1 79.3 %all-reduce.10.cloned.1.call-done = (f32[1,256,256]{2,1,0:T(8,128)}, f32[8,256,256]{2,1,0:T(8,128)}) async-done(((f32[1,256,256]{2,1,0:T(8,128)}, f32[8,256,256]{2,1,0:T(8,128)}), (f32[1,256,256]{2,1,0:T(8,128)}, f32[8,256,256]{2,1,0:T(8,128)})) %all-reduce.10.cloned.1.call-update) | async-done | bytes 2359312 | tf_op jit(solution)/shard_map/psum | solution.py:74
  332.5 2.0 fusion.8
  334.5 1.3 copy-done.1
  335.9 1.8 neg.10
  337.7 1.7 gather_fusion.11
  339.4 4.3 convolution_multiply_fusion
  346.2 1.3 copy-done.2
  347.7 28.5 %reduce-scatter.6.cloned.1.call-done = f32[1,256,256]{2,1,0:T(8,128)} async-done(((f32[8,256,256]{2,1,0:T(8,128)}), f32[1,256,256]{2,1,0:T(8,128)}) %reduce-scatter.6.cloned.1.call-update) | async-done | bytes 262160 | tf_op jit(solution)/shard_map/reduce_scatter | solution.py:99
  376.2 44.4 %reduce-scatter.8.cloned.1.call-done = f32[1,256,256]{2,1,0:T(8,128)} async-done(((f32[8,256,256]{2,1,0:T(8,128)}), f32[1,256,256]{2,1,0:T(8,128)}) %reduce-scatter.8.cloned.1.call-update) | async-done | bytes 262160 | tf_op jit(solution)/shard_map/reduce_scatter | solution.py:100
  420.6 1.9 constant_dynamic-slice_fusion.1
  422.5 1.9 constant_dynamic-slice_fusion
  424.3 37.3 %all-reduce.8.cloned.1.call-done = (f32[1,256,256]{2,1,0:T(8,128)}, f32[1,256,256]{2,1,0:T(8,128)}) async-done(((f32[1,256,256]{2,1,0:T(8,128)}, f32[1,256,256]{2,1,0:T(8,128)}), (f32[1,256,256]{2,1,0:T(8,128)}, f32[1,256,256]{2,1,0:T(8,128)})) %all-reduce.8.cloned.1.call-update) | async-done | bytes 524304 | tf_op jit(solution)/shard_map/psum | solution.py:102
  462.6 2.3 fusion.10
  (93 shorter events, 18.5 us)
Async XLA Ops:
  7.2 2.3 copy-start.13
  7.2 2.5 copy-start
  7.2 33.2 %all-gather.4.cloned.1.call-start = ((), (), s32[]{:S(2)}) async-start(), calls=%async_computation.3 | async-start | bytes 2359296 | tf_op jit(solution)/shard_map/all_gather | solution.py:45
  7.9 123.9 %all-reduce.6.cloned.1.call-start = ((), (), s32[]{:S(2)}) async-start(), calls=%async_computation.4 | async-start | bytes 4194304 | tf_op jit(solution)/shard_map/psum | solution.py:58
  45.5 3.2 copy-start.7
  45.5 115.0 %all-gather.6.cloned.1.call-start = ((), (), s32[]{:S(2)}) async-start(), calls=%async_computation.6 | async-start | bytes 2359296 | tf_op jit(solution)/shard_map/all_gather | solution.py:51
  46.3 143.9 %all-gather.8.cloned.1.call-start = ((), (), s32[]{:S(2)}) async-start(), calls=%async_computation.7 | async-start | bytes 2359296 | tf_op jit(solution)/shard_map/all_gather | solution.py:52
  46.9 187.5 %reduce-scatter.4.cloned.1.call-start = ((), (), s32[]{:S(2)}) async-start(), calls=%async_computation.5 | async-start | bytes 2359296 | tf_op jit(solution)/shard_map/reduce_scatter | solution.py:73
  133.6 1.7 copy-start.4
  142.3 1.3 copy-start.3
  143.7 187.7 %all-reduce.10.cloned.1.call-start = ((), (), s32[]{:S(2)}) async-start(), calls=%async_computation.11 | async-start | bytes 4718592 | tf_op jit(solution)/shard_map/psum | solution.py:74
  146.9 19.5 %copy-start.5 = (f32[8,256,256]{2,1,0:T(8,128)S(1)}, f32[8,256,256]{2,1,0:T(8,128)}, u32[]{:S(2)}) copy-start(f32[8,256,256]{2,1,0:T(8,128)} %copy-done.4) | copy-start | bytes 6291460
  192.9 47.6 %copy-start.14 = (s32[3]{0:T(128)S(1)}, s32[3]{0:T(128)}, u32[]{:S(2)}) copy-start(s32[3]{0:T(128)} %constant.171.clone.1) | copy-start | bytes 40
  234.4 141.8 %reduce-scatter.6.cloned.1.call-start = ((), (), s32[]{:S(2)}) async-start(), calls=%async_computation.8 | async-start | bytes 2359296 | tf_op jit(solution)/shard_map/reduce_scatter | solution.py:99
  332.5 5.2 %copy-start.9 = (f32[1,256,256]{2,1,0:T(8,128)}, f32[1,256,256]{2,1,0:T(8,128)S(1)}, u32[]{:S(2)}) copy-start(f32[1,256,256]{2,1,0:T(8,128)S(1)} %sub.32) | copy-start | bytes 786436
  334.5 1.3 copy-start.1
  335.9 84.7 %reduce-scatter.8.cloned.1.call-start = ((), (), s32[]{:S(2)}) async-start(), calls=%async_computation.9 | async-start | bytes 2359296 | tf_op jit(solution)/shard_map/reduce_scatter | solution.py:100
  337.7 1.7 copy-start.6
  343.7 1.3 copy-start.8
  346.2 1.3 copy-start.2
  347.6 115.0 %copy-start.10 = (f32[1,256,256]{2,1,0:T(8,128)S(1)}, f32[1,256,256]{2,1,0:T(8,128)}, u32[]{:S(2)}) copy-start(f32[1,256,256]{2,1,0:T(8,128)} %param.22) | copy-start | bytes 786436
  347.6 115.0 %copy-start.12 = (f32[1,256,256]{2,1,0:T(8,128)S(1)}, f32[1,256,256]{2,1,0:T(8,128)}, u32[]{:S(2)}) copy-start(f32[1,256,256]{2,1,0:T(8,128)} %param.23) | copy-start | bytes 786436
  347.6 114.0 %all-reduce.8.cloned.1.call-start = ((), (), s32[]{:S(2)}) async-start(), calls=%async_computation.10 | async-start | bytes 1048576 | tf_op jit(solution)/shard_map/psum | solution.py:102
  462.6 2.4 copy-start.11
Sparse Core Ops, SparseCore 0:
  9.9 30.4 all-gather.3
  45.7 86.1 all-reduce.5
  133.7 26.8 all-gather.5
  162.3 27.7 all-gather.7
  193.3 41.0 reduce-scatter.3
  236.7 94.6 all-reduce.9
  336.0 40.1 reduce-scatter.5
  379.5 41.0 reduce-scatter.7
  423.0 38.6 all-reduce.7
where the time goes:
time: 472 us
  waiting for transfers between devices  381 us (81%)
  matrix products  31 us (7%)
  local copies, waits for them, and re-layouts  27 us (6%)
  other arithmetic  16 us (3%)
  between operations  15.6 us (3%)
    psum x1, waiting for transfers between devices, body(): first_full = -lax.psum(first_terms, 'prow')  81.4 us
    psum x1, waiting for transfers between devices, body(): pivot_sum = lax.psum(pivot_part, 'prow')  79.3 us
    reduce_scatter x1, waiting for transfers between devices, body(): lax.psum_scatter(diag_terms, 'pcol', scatter_dimension=0, tiled=True)  44.4 us
    reduce_scatter x1, waiting for transfers between devices, body(): lax.psum_scatter(pivot_terms, 'pcol', scatter_dimension=0, tiled=True)  41.5 us
    psum x1, waiting for transfers between devices, body(): sum_cross, sum_diag = lax.psum((part_cross, part_diag), 'prow')  37.3 us
    all_gather x1, waiting for transfers between devices, body(): lowall = lax.all_gather(low_one, 'pcol', axis=0, tiled=True)  30 us
    reduce_scatter x1, waiting for transfers between devices, body(): lax.psum_scatter(cross_terms, 'pcol', scatter_dimension=0, tiled=True)  28.5 us
    all_gather x1, waiting for transfers between devices, body(): lax.all_gather(second_scaled_factor, 'pcol', axis=0, tiled=True)  23.2 us
  transfers between devices with their start and end apart: 9, of which 9 were waited for; matrix products, arithmetic and copies ran while one was open for 12% of the time, Pallas kernels for 0%

commit v1 on v0

--- a/solution.py
+++ b/solution.py
@@ -2,6 +2,17 @@
 import jax.numpy as jnp
 from jax import lax
 from jax.sharding import PartitionSpec as P
+
+
+def around_the_ring(x, axis, dim):
+    size = lax.axis_size(axis)
+    route = [(i, (i + 1) % size) for i in range(size)]
+    blocks = [x]
+    for far in range(1, size):
+        blocks = [lax.ppermute(blocks[0], axis, route), *blocks]
+    whole = jnp.concatenate(blocks, axis=dim)
+    turn = (lax.axis_index(axis) + 1) * blocks[-1].shape[dim]
+    return jnp.roll(whole, turn, axis=dim)
 
 
 def batched(left, right):
@@ -42,7 +53,7 @@
     zblocks = anc_inverse.reshape(supernode_block_width, owned, supernode_block_width).transpose(
         1, 0, 2
     )
-    lowall = lax.all_gather(low_one, "pcol", axis=0, tiled=True)
+    lowall = around_the_ring(low_one, "pcol", 0)
     total_one = lowall.shape[0]
     owned_slot_list = lax.dynamic_index_in_dim(pattern_one, my_row, 1, keepdims=False)
     chosen = jnp.take(zblocks, owned_slot_list - my_row * owned, axis=0)

time: 472 us -> 435 us (0.922)
  waiting for transfers between devices: 381 us -> 339 us
  local copies, waits for them, and re-layouts: 27 us -> 31.9 us
    ppermute x0 -> x7, waiting for transfers between devices: none -> 42.2 us  [around_the_ring(): blocks = [lax.ppermute(blocks[0], axis, route), *blocks]]
    all_gather x1 -> x0, waiting for transfers between devices: 30 us -> none  [body(): lowall = lax.all_gather(low_one, 'pcol', axis=0, tiled=True)]
    all_gather x1, waiting for transfers between devices: 23.2 us -> 0.03 us  [body(): lax.all_gather(second_scaled_factor, 'pcol', axis=0, tiled=True)]
    reduce_scatter x1, waiting for transfers between devices: 41.5 us -> 27.4 us  [body(): lax.psum_scatter(pivot_terms, 'pcol', scatter_dimension=0, tiled=True)]
    all_gather x1, waiting for transfers between devices: 13.7 us -> 0.03 us  [body(): lax.all_gather(low_two, 'pcol', axis=0, tiled=True)]
  transfers between devices with their start and end apart: 9 -> 15, of which waited for: 9 -> 13; matrix products, arithmetic and copies ran while one was open for 12% -> 14% of each run, Pallas kernels for 0% -> 0%
where the time goes in v1:
time: 435 us; the launch traced here: 434 us
  waiting for transfers between devices  339 us (78%)
  local copies, waits for them, and re-layouts  31.9 us (7%)
  matrix products  29 us (7%)
  between operations  17.4 us (4%)
  other arithmetic  15.5 us (4%)
    psum x1, waiting for transfers between devices, body(): first_full = -lax.psum(first_terms, 'prow')  82.6 us
    psum x1, waiting for transfers between devices, body(): pivot_sum = lax.psum(pivot_part, 'prow')  78.4 us
    reduce_scatter x1, waiting for transfers between devices, body(): lax.psum_scatter(diag_terms, 'pcol', scatter_dimension=0, tiled=True)  44.3 us
    ppermute x7, waiting for transfers between devices, around_the_ring(): blocks = [lax.ppermute(blocks[0], axis, route), *blocks]  42.2 us
    psum x1, waiting for transfers between devices, body(): sum_cross, sum_diag = lax.psum((part_cross, part_diag), 'prow')  35 us
    reduce_scatter x1, waiting for transfers between devices, body(): lax.psum_scatter(cross_terms, 'pcol', scatter_dimension=0, tiled=True)  28.1 us
    reduce_scatter x1, waiting for transfers between devices, body(): lax.psum_scatter(pivot_terms, 'pcol', scatter_dimension=0, tiled=True)  27.4 us
    dot_general x4, matrix products, batched_left_t(): jnp.einsum('kba,kbd->kad', left, right, precision=lax.Precision.HIGHEST)  14.6 us
  transfers between devices with their start and end apart: 15, of which 13 were waited for; matrix products, arithmetic and copies ran while one was open for 14% of the time, Pallas kernels for 0%

profile of v1, /device:TPU:0, one launch (start us, length us, event | category | flops | bytes accessed | tf_op | source)
XLA Modules:
  0.0 434.0 jit_solution(2823523064971785174)
XLA Ops:
  8.6 7.1 %collective-permute-done = f32[1,256,256]{2,1,0:T(8,128)S(1)} collective-permute-done((f32[1,256,256]{2,1,0:T(8,128)}, f32[1,256,256]{2,1,0:T(8,128)S(1)}, u32[]{:S(2)}, u32[]{:S(2)}) %collective-permute-start) | collective-permute-done | bytes 262176 | tf_op jit(solution)/shard_map/ppermute | solution.py:12
  15.7 6.7 %collective-permute-done.1 = f32[1,256,256]{2,1,0:T(8,128)S(1)} collective-permute-done((f32[1,256,256]{2,1,0:T(8,128)S(1)}, f32[1,256,256]{2,1,0:T(8,128)S(1)}, u32[]{:S(2)}, u32[]{:S(2)}) %collective-permute-start.1) | collective-permute-done | bytes 262176 | tf_op jit(solution)/shard_map/ppermute | solution.py:12
  22.4 6.7 %collective-permute-done.2 = f32[1,256,256]{2,1,0:T(8,128)S(1)} collective-permute-done((f32[1,256,256]{2,1,0:T(8,128)S(1)}, f32[1,256,256]{2,1,0:T(8,128)S(1)}, u32[]{:S(2)}, u32[]{:S(2)}) %collective-permute-start.2) | collective-permute-done | bytes 262176 | tf_op jit(solution)/shard_map/ppermute | solution.py:12
  29.1 6.7 %collective-permute-done.3 = f32[1,256,256]{2,1,0:T(8,128)S(1)} collective-permute-done((f32[1,256,256]{2,1,0:T(8,128)S(1)}, f32[1,256,256]{2,1,0:T(8,128)S(1)}, u32[]{:S(2)}, u32[]{:S(2)}) %collective-permute-start.3) | collective-permute-done | bytes 262176 | tf_op jit(solution)/shard_map/ppermute | solution.py:12
  35.8 6.7 %collective-permute-done.4 = f32[1,256,256]{2,1,0:T(8,128)S(1)} collective-permute-done((f32[1,256,256]{2,1,0:T(8,128)S(1)}, f32[1,256,256]{2,1,0:T(8,128)S(1)}, u32[]{:S(2)}, u32[]{:S(2)}) %collective-permute-start.4) | collective-permute-done | bytes 262176 | tf_op jit(solution)/shard_map/ppermute | solution.py:12
  44.1 5.1 %collective-permute-done.5 = f32[1,256,256]{2,1,0:T(8,128)S(1)} collective-permute-done((f32[1,256,256]{2,1,0:T(8,128)S(1)}, f32[1,256,256]{2,1,0:T(8,128)S(1)}, u32[]{:S(2)}, u32[]{:S(2)}) %collective-permute-start.5) | collective-permute-done | bytes 262176 | tf_op jit(solution)/shard_map/ppermute | solution.py:12
  50.7 2.0 gather_fusion.3
  52.7 3.2 collective-permute-done.6
  57.9 3.5 fusion.2
  64.5 1.7 gather_fusion.5
  66.2 82.6 %all-reduce.6.cloned.1.call-done = f32[8,256,256]{2,1,0:T(8,128)} async-done(((f32[8,256,256]{2,1,0:T(8,128)}), f32[8,256,256]{2,1,0:T(8,128)}) %all-reduce.6.cloned.1.call-update) | async-done | bytes 2097168 | tf_op jit(solution)/shard_map/psum | solution.py:69
  148.8 1.8 neg.9
  150.6 1.7 gather_fusion.6
  152.3 4.5 %convolution_multiply_fusion.2 = f32[4,256,256]{2,1,0:T(8,128)} fusion(f32[4,256,256]{2,1,0:T(8,128)} %gather_fusion.6, f32[4,256,256]{2,1,0:T(8,128)} %gather_fusion.5, f32[4]{0:T(128)S(1)} %select_convert_fusion.1, pred[4]{0:T(512)(128)(4,1)S(1)} %get-tuple-element.71), kind=kOutput, calls=%fused_computation.21 | convolution fusion | flops 806092800 | bytes 3145748 | tf_op jit(solution)/shard_map/kba,kbd->kad/dot_general | solution.py:23
  157.0 2.3 scatter_fusion
  161.8 2.0 gather_fusion.7
  163.9 6.1 %fusion = f32[8,256,256]{2,1,0:T(8,128)} fusion(f32[8,256,256]{2,1,0:T(8,128)} %all-gather.3.cloned.1.call-done, f32[8,256,256]{2,1,0:T(8,128)} %gather_fusion.7, pred[8]{0:T(512)(128)(4,1)S(1)} %compare_and_fusion.2), kind=kOutput, calls=%fused_computation.15 | convolution fusion | flops 1611137024 | bytes 6291464 | tf_op jit(solution)/shard_map/kab,kbd->kad/dot_general | solution.py:19
  170.6 2.8 fusion.4
  173.4 27.4 %reduce-scatter.4.cloned.1.call-done = f32[1,256,256]{2,1,0:T(8,128)} async-done(((f32[8,256,256]{2,1,0:T(8,128)}), f32[1,256,256]{2,1,0:T(8,128)}) %reduce-scatter.4.cloned.1.call-update) | async-done | bytes 262160 | tf_op jit(solution)/shard_map/reduce_scatter | solution.py:84
  207.6 3.2 gather_fusion.10
  212.4 3.5 convolution_multiply_fusion.1
  217.2 78.4 %all-reduce.10.cloned.1.call-done = (f32[1,256,256]{2,1,0:T(8,128)}, f32[8,256,256]{2,1,0:T(8,128)}) async-done(((f32[1,256,256]{2,1,0:T(8,128)}, f32[8,256,256]{2,1,0:T(8,128)}), (f32[1,256,256]{2,1,0:T(8,128)}, f32[8,256,256]{2,1,0:T(8,128)})) %all-reduce.10.cloned.1.call-update) | async-done | bytes 2359312 | tf_op jit(solution)/shard_map/psum | solution.py:85
  296.7 2.0 fusion.8
  300.2 1.8 neg.10
  302.0 1.6 gather_fusion.11
  304.0 4.3 convolution_multiply_fusion
  312.1 28.1 %reduce-scatter.6.cloned.1.call-done = f32[1,256,256]{2,1,0:T(8,128)} async-done(((f32[8,256,256]{2,1,0:T(8,128)}), f32[1,256,256]{2,1,0:T(8,128)}) %reduce-scatter.6.cloned.1.call-update) | async-done | bytes 262160 | tf_op jit(solution)/shard_map/reduce_scatter | solution.py:110
  340.2 44.3 %reduce-scatter.8.cloned.1.call-done = f32[1,256,256]{2,1,0:T(8,128)} async-done(((f32[8,256,256]{2,1,0:T(8,128)}), f32[1,256,256]{2,1,0:T(8,128)}) %reduce-scatter.8.cloned.1.call-update) | async-done | bytes 262160 | tf_op jit(solution)/shard_map/reduce_scatter | solution.py:111
  384.6 1.9 constant_dynamic-slice_fusion.1
  386.4 1.9 constant_dynamic-slice_fusion
  388.3 35.0 %all-reduce.8.cloned.1.call-done = (f32[1,256,256]{2,1,0:T(8,128)}, f32[1,256,256]{2,1,0:T(8,128)}) async-done(((f32[1,256,256]{2,1,0:T(8,128)}, f32[1,256,256]{2,1,0:T(8,128)}), (f32[1,256,256]{2,1,0:T(8,128)}, f32[1,256,256]{2,1,0:T(8,128)})) %all-reduce.8.cloned.1.call-update) | async-done | bytes 524304 | tf_op jit(solution)/shard_map/psum | solution.py:113
  424.3 2.3 fusion.10
  (123 shorter events, 27.9 us)
Async XLA Ops:
  8.0 140.8 %all-reduce.6.cloned.1.call-start = ((), (), s32[]{:S(2)}) async-start(), calls=%async_computation.3 | async-start | bytes 4194304 | tf_op jit(solution)/shard_map/psum | solution.py:69
  8.0 7.7 %collective-permute-start = (f32[1,256,256]{2,1,0:T(8,128)}, f32[1,256,256]{2,1,0:T(8,128)S(1)}, u32[]{:S(2)}, u32[]{:S(2)}) collective-permute-start(f32[1,256,256]{2,1,0:T(8,128)} %param.19), channel_id=1, source_target_pairs={{0,1},{1,2},{2,3},{3,4},{4,5},{5,6},{6,7},{7,0},{8,9},{9,10},{10,1... | collective-permute-start | bytes 786440 | tf_op jit(solution)/shard_map/ppermute | solution.py:12
  15.7 6.7 %collective-permute-start.1 = (f32[1,256,256]{2,1,0:T(8,128)S(1)}, f32[1,256,256]{2,1,0:T(8,128)S(1)}, u32[]{:S(2)}, u32[]{:S(2)}) collective-permute-start(f32[1,256,256]{2,1,0:T(8,128)S(1)} %collective-permute-done), channel_id=1, source_target_pairs={{0,1},{1,2},{2,3},{3,4},{4,5},{5,6},{6,7},{7,0},{8,9},{9,10},{10,1... | collective-permute-start | bytes 786440 | tf_op jit(solution)/shard_map/ppermute | solution.py:12
  22.4 6.7 %collective-permute-start.2 = (f32[1,256,256]{2,1,0:T(8,128)S(1)}, f32[1,256,256]{2,1,0:T(8,128)S(1)}, u32[]{:S(2)}, u32[]{:S(2)}) collective-permute-start(f32[1,256,256]{2,1,0:T(8,128)S(1)} %collective-permute-done.1), channel_id=1, source_target_pairs={{0,1},{1,2},{2,3},{3,4},{4,5},{5,6},{6,7},{7,0},{8,9},{9,10},{10,1... | collective-permute-start | bytes 786440 | tf_op jit(solution)/shard_map/ppermute | solution.py:12
  29.1 6.7 %collective-permute-start.3 = (f32[1,256,256]{2,1,0:T(8,128)S(1)}, f32[1,256,256]{2,1,0:T(8,128)S(1)}, u32[]{:S(2)}, u32[]{:S(2)}) collective-permute-start(f32[1,256,256]{2,1,0:T(8,128)S(1)} %collective-permute-done.2), channel_id=1, source_target_pairs={{0,1},{1,2},{2,3},{3,4},{4,5},{5,6},{6,7},{7,0},{8,9},{9,10},{10,1... | collective-permute-start | bytes 786440 | tf_op jit(solution)/shard_map/ppermute | solution.py:12
  35.8 6.7 %collective-permute-start.4 = (f32[1,256,256]{2,1,0:T(8,128)S(1)}, f32[1,256,256]{2,1,0:T(8,128)S(1)}, u32[]{:S(2)}, u32[]{:S(2)}) collective-permute-start(f32[1,256,256]{2,1,0:T(8,128)S(1)} %collective-permute-done.3), channel_id=1, source_target_pairs={{0,1},{1,2},{2,3},{3,4},{4,5},{5,6},{6,7},{7,0},{8,9},{9,10},{10,1... | collective-permute-start | bytes 786440 | tf_op jit(solution)/shard_map/ppermute | solution.py:12
  42.5 6.7 %collective-permute-start.5 = (f32[1,256,256]{2,1,0:T(8,128)S(1)}, f32[1,256,256]{2,1,0:T(8,128)S(1)}, u32[]{:S(2)}, u32[]{:S(2)}) collective-permute-start(f32[1,256,256]{2,1,0:T(8,128)S(1)} %collective-permute-done.4), channel_id=1, source_target_pairs={{0,1},{1,2},{2,3},{3,4},{4,5},{5,6},{6,7},{7,0},{8,9},{9,10},{10,1... | collective-permute-start | bytes 786440 | tf_op jit(solution)/shard_map/ppermute | solution.py:12
  49.2 6.7 %collective-permute-start.6 = (f32[1,256,256]{2,1,0:T(8,128)S(1)}, f32[1,256,256]{2,1,0:T(8,128)S(1)}, u32[]{:S(2)}, u32[]{:S(2)}) collective-permute-start(f32[1,256,256]{2,1,0:T(8,128)S(1)} %collective-permute-done.5), channel_id=1, source_target_pairs={{0,1},{1,2},{2,3},{3,4},{4,5},{5,6},{6,7},{7,0},{8,9},{9,10},{10,1... | collective-permute-start | bytes 786440 | tf_op jit(solution)/shard_map/ppermute | solution.py:12
  52.7 3.4 copy-start.13
  56.4 1.6 copy-start.7
  61.5 102.4 %all-gather.3.cloned.1.call-start = ((), (), s32[]{:S(2)}) async-start(), calls=%async_computation.5 | async-start | bytes 2359296 | tf_op jit(solution)/shard_map/all_gather | solution.py:62
  62.1 108.6 %all-gather.5.cloned.1.call-start = ((), (), s32[]{:S(2)}) async-start(), calls=%async_computation.6 | async-start | bytes 2359296 | tf_op jit(solution)/shard_map/all_gather | solution.py:63
  62.6 138.1 %reduce-scatter.4.cloned.1.call-start = ((), (), s32[]{:S(2)}) async-start(), calls=%async_computation.4 | async-start | bytes 2359296 | tf_op jit(solution)/shard_map/reduce_scatter | solution.py:84
  150.6 1.7 copy-start.4
  157.0 3.8 copy-start
  159.3 1.3 copy-start.3
  160.7 135.0 %all-reduce.10.cloned.1.call-start = ((), (), s32[]{:S(2)}) async-start(), calls=%async_computation.10 | async-start | bytes 4718592 | tf_op jit(solution)/shard_map/psum | solution.py:85
  163.9 6.1 %copy-start.5 = (f32[8,256,256]{2,1,0:T(8,128)S(1)}, f32[8,256,256]{2,1,0:T(8,128)}, u32[]{:S(2)}) copy-start(f32[8,256,256]{2,1,0:T(8,128)} %copy-done.4) | copy-start | bytes 6291460
  173.4 33.5 %copy-start.15 = (s32[3]{0:T(128)S(1)}, s32[3]{0:T(128)}, u32[]{:S(2)}) copy-start(s32[3]{0:T(128)} %constant.191.clone.1) | copy-start | bytes 40
  200.8 139.4 %reduce-scatter.6.cloned.1.call-start = ((), (), s32[]{:S(2)}) async-start(), calls=%async_computation.7 | async-start | bytes 2359296 | tf_op jit(solution)/shard_map/reduce_scatter | solution.py:110
  296.7 5.2 %copy-start.10 = (f32[1,256,256]{2,1,0:T(8,128)}, f32[1,256,256]{2,1,0:T(8,128)S(1)}, u32[]{:S(2)}) copy-start(f32[1,256,256]{2,1,0:T(8,128)S(1)} %sub.37) | copy-start | bytes 786436
  298.7 1.3 copy-start.1
  300.1 84.4 %reduce-scatter.8.cloned.1.call-start = ((), (), s32[]{:S(2)}) async-start(), calls=%async_computation.8 | async-start | bytes 2359296 | tf_op jit(solution)/shard_map/reduce_scatter | solution.py:111
  301.9 1.6 copy-start.8
  301.9 2.0 copy-start.6
  308.2 1.3 copy-start.9
  310.7 1.3 copy-start.2
  312.0 112.3 %copy-start.11 = (f32[1,256,256]{2,1,0:T(8,128)S(1)}, f32[1,256,256]{2,1,0:T(8,128)}, u32[]{:S(2)}) copy-start(f32[1,256,256]{2,1,0:T(8,128)} %param.22) | copy-start | bytes 786436
  312.0 112.3 %copy-start.14 = (f32[1,256,256]{2,1,0:T(8,128)S(1)}, f32[1,256,256]{2,1,0:T(8,128)}, u32[]{:S(2)}) copy-start(f32[1,256,256]{2,1,0:T(8,128)} %param.23) | copy-start | bytes 786436
  312.1 111.3 %all-reduce.8.cloned.1.call-start = ((), (), s32[]{:S(2)}) async-start(), calls=%async_computation.9 | async-start | bytes 1048576 | tf_op jit(solution)/shard_map/psum | solution.py:113
  424.3 2.4 copy-start.12
Sparse Core Ops, SparseCore 0:
  61.6 87.1 all-reduce.5
  200.9 94.6 all-reduce.9
  384.7 38.5 all-reduce.7
Sparse Core Ops, SparseCore 1:
  63.9 28.7 all-gather.2
  94.4 27.6 all-gather.4
  160.8 40.0 reduce-scatter.3
  300.2 40.0 reduce-scatter.5
  343.5 41.0 reduce-scatter.7
